TPU v7x, 512 devices: a whole 4x8x8 slice. The times are simulated.
512 devices in a mesh: cam: 128 (over y, z, core), proj: 4 (over x).
Axes of the slice: x: 4, y: 8, z: 8, core: 2. Of those that a mesh axis runs over, the one named last changes fastest.
Arguments:
- transport: bfloat16 [65536, 16384], P('cam', 'proj'), may hold values from -0.09375 to 0.09375
- test_panel: bfloat16 [16384, 32], P(('proj', 'cam')), may hold values from -6 to 6
Outputs:
- basis: float32 [65536, 32], P('cam')
- coimage: float32 [16384, 32], P(('proj', 'cam'))
All inputs are finite; a program needn't handle non-finite values.
Results may differ from a plain program's by a relative error of at most 0.0027.
Values may be sent and summed in bfloat16 or wider, within the bound.
No kernel may reach another device: no remote copies, remote signals or barrier semaphores. Data moves between devices by JAX's collectives and lax.ppermute only.
A program may use at most 64 MiB of HBM per device.

v0:
```python
import jax
import jax.numpy as jnp
from jax import lax
from jax.sharding import PartitionSpec as P

ITERS = 2


def small_gram(block):
    return jnp.dot(
        block.T, block, precision=lax.Precision.HIGHEST, preferred_element_type=jnp.float32
    )


def apply_factor(gram, block):
    lower = jnp.linalg.cholesky(gram)
    return jax.scipy.linalg.solve_triangular(lower, block.T, lower=True).T


def on_device(transport, test_panel):
    rows_here = transport.shape[0]
    total_rows = rows_here * lax.axis_size("cam")
    panel_piece = test_panel
    basis = None
    coimage = None
    for step in range(ITERS):
        partial_sketch = jnp.dot(
            transport,
            lax.all_gather(panel_piece, "cam", axis=0, tiled=True),
            preferred_element_type=jnp.float32,
        )
        sketch = lax.psum(partial_sketch, "proj")
        gram = lax.psum(small_gram(sketch), "cam") / total_rows
        basis = apply_factor(gram, sketch)
        basis_low = basis.astype(jnp.bfloat16)
        last = step + 1 == ITERS
        coimage = lax.psum_scatter(
            lax.dot_general(
                transport, basis_low, (((0,), (0,)), ((), ())), preferred_element_type=jnp.float32
            ),
            "cam",
            scatter_dimension=0,
            tiled=True,
        )
        if not last:
            panel_piece = coimage.astype(jnp.bfloat16)
    return (basis, coimage)


def solution(mesh):
    placed = (P("cam", "proj"), P(("proj", "cam"), None))
    return jax.shard_map(
        on_device,
        mesh=mesh,
        in_specs=placed,
        out_specs=(P("cam", None), P(("proj", "cam"), None)),
        check_vma=False,
    )
```

profile of v0, /device:TPU:2, one launch (start us, length us, event | category | flops | bytes accessed | tf_op | source)
XLA Modules:
  0.0 1628.0 jit_solution(12464336792124813939)
XLA Ops:
  7.2 57.9 %all_gather.6 = bf16[4096,32]{1,0:T(8,128)(2,1)S(1)} all-gather(bf16[32,32]{1,0:T(8,128)(2,1)} %param.6), channel_id=1, replica_groups=mesh['cam'=128,'proj'=4] {'cam'}, dimensions={0}, use_global_device_ids=true | all-gather | bytes 264192 | tf_op jit(solution)/shard_map/all_gather | solution.py:29
  65.1 4.2 fusion.11
  69.3 46.1 %all-reduce.3.cloned.1.call-done = f32[512,32]{0,1:T(8,128)} async-done(((f32[512,32]{0,1:T(8,128)}), f32[512,32]{0,1:T(8,128)}) %all-reduce.3.cloned.1.call-update) | async-done | bytes 65552 | tf_op jit(solution)/shard_map/psum | solution.py:32
  115.4 1.1 fusion.12
  116.5 494.6 %psum.29 = f32[32,32]{0,1:T(8,128)S(1)} all-reduce(f32[32,32]{0,1:T(8,128)S(1)} %fusion.12), channel_id=1, replica_groups=mesh['cam'=128,'proj'=4] {'cam'}, use_global_device_ids=true, to_apply=%region_1.0 | all-reduce | flops 1024 | bytes 8192 | tf_op jit(solution)/shard_map/psum | solution.py:33
  611.2 2.9 cholesky.44
  614.8 0.7 fusion.3
  615.5 2.4 custom-call.6
  617.9 1.1 convolution_convert_fusion
  619.1 3.0 convolution_bitcast_fusion.1
  622.1 2.0 copy.17
  624.1 193.1 %reduce-scatter.7.cloned.1.call-done = f32[32,32]{1,0:T(8,128)} async-done(((f32[4096,32]{1,0:T(8,128)}), f32[32,32]{1,0:T(8,128)}) %reduce-scatter.7.cloned.1.call-update) | async-done | bytes 4112
  817.2 0.8 copy.18
  818.1 49.0 %all_gather.7 = bf16[4096,32]{1,0:T(8,128)(2,1)S(1)} all-gather(bf16[32,32]{1,0:T(8,128)(2,1)S(1)} %copy.11), channel_id=1, replica_groups=mesh['cam'=128,'proj'=4] {'cam'}, dimensions={0}, use_global_device_ids=true | all-gather | bytes 264192 | tf_op jit(solution)/shard_map/all_gather | solution.py:29
  867.1 4.2 convolution_bitcast_fusion.3
  871.3 48.4 %all-reduce.5.cloned.1.call-done = f32[512,32]{0,1:T(8,128)} async-done(((f32[512,32]{0,1:T(8,128)}), f32[512,32]{0,1:T(8,128)}) %all-reduce.5.cloned.1.call-update) | async-done | bytes 65552 | tf_op jit(solution)/shard_map/psum | solution.py:32
  919.8 1.1 fusion.13
  920.9 494.6 %psum.31 = f32[32,32]{0,1:T(8,128)S(1)} all-reduce(f32[32,32]{0,1:T(8,128)S(1)} %fusion.13), channel_id=1, replica_groups=mesh['cam'=128,'proj'=4] {'cam'}, use_global_device_ids=true, to_apply=%region_6.9 | all-reduce | flops 1024 | bytes 8192 | tf_op jit(solution)/shard_map/psum | solution.py:33
  1415.6 2.9 cholesky.55
  1419.8 2.4 custom-call.7
  1422.3 1.1 convolution_bitcast_fusion.2
  1423.4 3.0 convolution_bitcast_fusion
  1426.4 2.0 copy.19
  1428.5 193.0 %reduce-scatter.9.cloned.1.call-done = f32[32,32]{1,0:T(8,128)} async-done(((f32[4096,32]{1,0:T(8,128)}), f32[32,32]{1,0:T(8,128)}) %reduce-scatter.9.cloned.1.call-update) | async-done | bytes 4112
  (22 shorter events, 2.5 us)
Async XLA Ops:
  7.2 108.3 %all-reduce.3.cloned.1.call-start = ((), (), s32[]{:S(2)}) async-start(), calls=%async_computation.2 | async-start | bytes 131072 | tf_op jit(solution)/shard_map/psum | solution.py:32
  69.3 747.9 %reduce-scatter.7.cloned.1.call-start = ((), (), s32[]{:S(2)}) async-start(), calls=%async_computation.4 | async-start | bytes 2113536
  624.1 295.7 %all-reduce.5.cloned.1.call-start = ((), (), s32[]{:S(2)}) async-start(), calls=%async_computation.3 | async-start | bytes 131072 | tf_op jit(solution)/shard_map/psum | solution.py:32
  871.3 750.2 %reduce-scatter.9.cloned.1.call-start = ((), (), s32[]{:S(2)}) async-start(), calls=%async_computation.5 | async-start | bytes 2113536
  1423.4 5.0 copy-start
Sparse Core Ops, SparseCore 0:
  69.4 45.9 all-reduce.2
  624.2 192.9 reduce-scatter.6
  871.4 48.3 all-reduce.4
  1428.6 192.8 reduce-scatter.8
where the time goes:
time: 1630 us
  blocking collectives  1100 us (67%)
  waiting for transfers between devices  481 us (30%)
  matrix products  18.9 us (1%)
    psum x2, blocking collectives, on_device(): gram = lax.psum(small_gram(sketch), 'cam') / total_rows  989 us
    unnamed x6, waiting for transfers between devices  386 us
    all_gather x2, blocking collectives, on_device(): lax.all_gather(panel_piece, 'cam', axis=0, tiled=True)  107 us
    psum x2, waiting for transfers between devices, on_device(): sketch = lax.psum(partial_sketch, 'proj')  94.5 us
  transfers between devices with their start and end apart: 4, of which 4 were waited for; matrix products, arithmetic and copies ran while one was open for 0% of the time, Pallas kernels for 0%

commit v1 on v0

--- a/solution.py
+++ b/solution.py
@@ -4,6 +4,13 @@
 from jax.sharding import PartitionSpec as P
 
 ITERS = 2
+
+
+def exchange_gather(x, axis, dim):
+    devices = lax.axis_size(axis)
+    shards = jnp.stack([x for _ in range(devices)])
+    shards = lax.all_to_all(shards, axis, split_axis=0, concat_axis=0)
+    return jnp.concatenate(shards, axis=dim)
 
 
 def small_gram(block):
@@ -25,9 +32,7 @@
     coimage = None
     for step in range(ITERS):
         partial_sketch = jnp.dot(
-            transport,
-            lax.all_gather(panel_piece, "cam", axis=0, tiled=True),
-            preferred_element_type=jnp.float32,
+            transport, exchange_gather(panel_piece, "cam", 0), preferred_element_type=jnp.float32
         )
         sketch = lax.psum(partial_sketch, "proj")
         gram = lax.psum(small_gram(sketch), "cam") / total_rows

time: 1630 us -> 1570 us (0.963)
  blocking collectives: 1100 us -> 1050 us
    all_gather x2 -> x0, blocking collectives: 107 us -> none  [on_device(): lax.all_gather(panel_piece, 'cam', axis=0, tiled=True)]
    all_to_all x0 -> x2, blocking collectives: none -> 57.9 us  [exchange_gather(): shards = lax.all_to_all(shards, axis, split_axis=0, concat_axis=0)]
where the time goes in v1:
time: 1570 us
  blocking collectives  1050 us (67%)
  waiting for transfers between devices  472 us (30%)
  matrix products  18.9 us (1%)
    psum x2, blocking collectives, on_device(): gram = lax.psum(small_gram(sketch), 'cam') / total_rows  989 us
    unnamed x6, waiting for transfers between devices  386 us
    psum x2, waiting for transfers between devices, on_device(): sketch = lax.psum(partial_sketch, 'proj')  85.3 us
    all_to_all x2, blocking collectives, exchange_gather(): shards = lax.all_to_all(shards, axis, split_axis=0, concat_axis=0)  57.9 us
  transfers between devices with their start and end apart: 4, of which 4 were waited for; matrix products, arithmetic and copies ran while one was open for 0% of the time, Pallas kernels for 0%

profile of v1, /device:TPU:2, one launch (start us, length us, event | category | flops | bytes accessed | tf_op | source)
XLA Modules:
  0.0 1573.5 jit_solution(11671873639737771188)
XLA Ops:
  7.2 0.8 stack.4
  8.0 0.8 reshape.28
  8.9 32.7 %all_to_all.10 = bf16[128,2,512]{2,1,0:T(2,128)(2,1)S(1)} all-to-all(bf16[128,2,512]{2,1,0:T(2,128)(2,1)S(1)} %reshape.28), channel_id=1, replica_groups=mesh['cam'=128,'proj'=4] {'cam'}, dimensions={0} | all-to-all | bytes 524288 | tf_op jit(solution)/shard_map/all_to_all | solution.py:12
  42.1 4.2 fusion.11
  46.4 42.7 %all-reduce.3.cloned.1.call-done = f32[512,32]{0,1:T(8,128)} async-done(((f32[512,32]{0,1:T(8,128)}), f32[512,32]{0,1:T(8,128)}) %all-reduce.3.cloned.1.call-update) | async-done | bytes 65552 | tf_op jit(solution)/shard_map/psum | solution.py:37
  89.0 1.1 fusion.12
  90.1 494.6 %psum.29 = f32[32,32]{0,1:T(8,128)S(1)} all-reduce(f32[32,32]{0,1:T(8,128)S(1)} %fusion.12), channel_id=1, replica_groups=mesh['cam'=128,'proj'=4] {'cam'}, use_global_device_ids=true, to_apply=%region_1.0 | all-reduce | flops 1024 | bytes 8192 | tf_op jit(solution)/shard_map/psum | solution.py:38
  584.8 2.9 cholesky.44
  589.1 2.4 custom-call.6
  591.5 1.1 convolution_convert_fusion
  592.7 3.0 convolution_bitcast_fusion.1
  595.7 2.0 copy.18
  597.7 193.1 %reduce-scatter.7.cloned.1.call-done = f32[32,32]{1,0:T(8,128)} async-done(((f32[4096,32]{1,0:T(8,128)}), f32[32,32]{1,0:T(8,128)}) %reduce-scatter.7.cloned.1.call-update) | async-done | bytes 4112
  792.6 25.2 %all_to_all.11 = bf16[128,2,512]{2,1,0:T(2,128)(2,1)S(1)} all-to-all(bf16[128,2,512]{2,1,0:T(2,128)(2,1)S(1)} %reshape.30), channel_id=1, replica_groups=mesh['cam'=128,'proj'=4] {'cam'}, dimensions={0} | all-to-all | bytes 524288 | tf_op jit(solution)/shard_map/all_to_all | solution.py:12
  818.3 4.2 convolution_bitcast_fusion.3
  822.6 42.6 %all-reduce.5.cloned.1.call-done = f32[512,32]{0,1:T(8,128)} async-done(((f32[512,32]{0,1:T(8,128)}), f32[512,32]{0,1:T(8,128)}) %all-reduce.5.cloned.1.call-update) | async-done | bytes 65552 | tf_op jit(solution)/shard_map/psum | solution.py:37
  865.3 1.1 fusion.13
  866.4 494.6 %psum.31 = f32[32,32]{0,1:T(8,128)S(1)} all-reduce(f32[32,32]{0,1:T(8,128)S(1)} %fusion.13), channel_id=1, replica_groups=mesh['cam'=128,'proj'=4] {'cam'}, use_global_device_ids=true, to_apply=%region_6.9 | all-reduce | flops 1024 | bytes 8192 | tf_op jit(solution)/shard_map/psum | solution.py:38
  1361.1 2.9 cholesky.55
  1365.3 2.4 custom-call.7
  1367.8 1.1 convolution_bitcast_fusion.2
  1368.9 3.0 convolution_bitcast_fusion
  1371.9 2.0 copy.20
  1373.9 193.0 %reduce-scatter.9.cloned.1.call-done = f32[32,32]{1,0:T(8,128)} async-done(((f32[4096,32]{1,0:T(8,128)}), f32[32,32]{1,0:T(8,128)}) %reduce-scatter.9.cloned.1.call-update) | async-done | bytes 4112
  (28 shorter events, 5.9 us)
Async XLA Ops:
  7.2 81.9 %all-reduce.3.cloned.1.call-start = ((), (), s32[]{:S(2)}) async-start(), calls=%async_computation.4 | async-start | bytes 131072 | tf_op jit(solution)/shard_map/psum | solution.py:37
  46.3 744.5 %reduce-scatter.7.cloned.1.call-start = ((), (), s32[]{:S(2)}) async-start(), calls=%async_computation.6 | async-start | bytes 2113536
  597.7 267.6 %all-reduce.5.cloned.1.call-start = ((), (), s32[]{:S(2)}) async-start(), calls=%async_computation.5 | async-start | bytes 131072 | tf_op jit(solution)/shard_map/psum | solution.py:37
  822.6 744.4 %reduce-scatter.9.cloned.1.call-start = ((), (), s32[]{:S(2)}) async-start(), calls=%async_computation.7 | async-start | bytes 2113536
  1368.9 5.0 copy-start
Sparse Core Ops, SparseCore 0:
  46.4 42.5 all-reduce.2
  597.8 192.9 reduce-scatter.6
  822.7 42.5 all-reduce.4
  1374.1 192.8 reduce-scatter.8

commit v2 on v0

--- a/solution.py
+++ b/solution.py
@@ -29,7 +29,8 @@
             lax.all_gather(panel_piece, "cam", axis=0, tiled=True),
             preferred_element_type=jnp.float32,
         )
-        sketch = lax.psum(partial_sketch, "proj")
+        shards = lax.all_gather(partial_sketch, "proj")
+        sketch = jnp.sum(shards, axis=0)
         gram = lax.psum(small_gram(sketch), "cam") / total_rows
         basis = apply_factor(gram, sketch)
         basis_low = basis.astype(jnp.bfloat16)

time: 1630 us -> 1550 us (0.951)
  waiting for transfers between devices: 481 us -> 387 us
    psum x2 -> x0, waiting for transfers between devices: 94.5 us -> none  [on_device(): sketch = lax.psum(partial_sketch, 'proj')]
    all_gather x0 -> x2, blocking collectives: none -> 25.3 us  [on_device(): shards = lax.all_gather(partial_sketch, 'proj')]
    unnamed x6 -> x4, waiting for transfers between devices: 386 us -> 387 us
  transfers between devices with their start and end apart: 4 -> 2, of which waited for: 4 -> 2; matrix products, arithmetic and copies ran while one was open for 0% -> 0% of each run, Pallas kernels for 0% -> 0%
where the time goes in v2:
time: 1550 us
  blocking collectives  1110 us (72%)
  waiting for transfers between devices  387 us (25%)
    psum x2, blocking collectives, on_device(): gram = lax.psum(small_gram(sketch), 'cam') / total_rows  982 us
    unnamed x4, waiting for transfers between devices  387 us
    all_gather x2, blocking collectives, on_device(): lax.all_gather(panel_piece, 'cam', axis=0, tiled=True)  107 us
  transfers between devices with their start and end apart: 2, of which 2 were waited for; matrix products, arithmetic and copies ran while one was open for 0% of the time, Pallas kernels for 0%

profile of v2, /device:TPU:2, one launch (start us, length us, event | category | flops | bytes accessed | tf_op | source)
XLA Modules:
  0.0 1547.9 jit_solution(13389474285750706124)
XLA Ops:
  7.2 57.9 %all_gather.18 = bf16[4096,32]{1,0:T(8,128)(2,1)S(1)} all-gather(bf16[32,32]{1,0:T(8,128)(2,1)} %param.6), channel_id=1, replica_groups=mesh['cam'=128,'proj'=4] {'cam'}, dimensions={0}, use_global_device_ids=true | all-gather | bytes 264192 | tf_op jit(solution)/shard_map/all_gather | solution.py:29
  65.1 3.5 fusion.11
  68.6 12.6 all-gather
  81.7 490.9 %psum.14 = f32[32,32]{0,1:T(8,128)S(1)} all-reduce(f32[32,32]{0,1:T(8,128)S(1)} %fusion.12), channel_id=1, replica_groups=mesh['cam'=128,'proj'=4] {'cam'}, use_global_device_ids=true, to_apply=%region_1.0 | all-reduce | flops 1024 | bytes 8192 | tf_op jit(solution)/shard_map/psum | solution.py:34
  572.7 2.9 cholesky.44
  575.6 0.6 compare_reduce_fusion.1
  576.3 0.7 fusion.3
  576.9 2.4 custom-call.6
  579.4 0.3 convolution_convert_fusion
  579.7 3.0 convolution_bitcast_fusion.1
  582.7 2.0 copy.17
  584.7 193.5 %reduce-scatter.7.cloned.1.call-done = f32[32,32]{1,0:T(8,128)} async-done(((f32[4096,32]{1,0:T(8,128)}), f32[32,32]{1,0:T(8,128)}) %reduce-scatter.7.cloned.1.call-update) | async-done | bytes 4112
  778.2 0.8 copy.18
  779.1 49.0 %all_gather.21 = bf16[4096,32]{1,0:T(8,128)(2,1)S(1)} all-gather(bf16[32,32]{1,0:T(8,128)(2,1)S(1)} %copy.11), channel_id=1, replica_groups=mesh['cam'=128,'proj'=4] {'cam'}, dimensions={0}, use_global_device_ids=true | all-gather | bytes 264192 | tf_op jit(solution)/shard_map/all_gather | solution.py:29
  828.1 3.6 convolution_bitcast_fusion.3
  831.6 12.7 all-gather.1
  844.9 490.9 %psum.15 = f32[32,32]{0,1:T(8,128)S(1)} all-reduce(f32[32,32]{0,1:T(8,128)S(1)} %fusion.13), channel_id=1, replica_groups=mesh['cam'=128,'proj'=4] {'cam'}, use_global_device_ids=true, to_apply=%region_6.9 | all-reduce | flops 1024 | bytes 8192 | tf_op jit(solution)/shard_map/psum | solution.py:34
  1335.8 2.9 cholesky.55
  1338.8 0.6 compare_reduce_fusion
  1339.4 0.7 fusion.4
  1340.1 2.4 custom-call.7
  1342.8 3.0 convolution_bitcast_fusion
  1345.8 2.0 copy.19
  1347.9 193.2 %reduce-scatter.9.cloned.1.call-done = f32[32,32]{1,0:T(8,128)} async-done(((f32[4096,32]{1,0:T(8,128)}), f32[32,32]{1,0:T(8,128)}) %reduce-scatter.9.cloned.1.call-update) | async-done | bytes 4112
  (22 shorter events, 1.8 us)
Async XLA Ops:
  7.2 771.0 %reduce-scatter.7.cloned.1.call-start = ((), (), s32[]{:S(2)}) async-start(), calls=%async_computation.2 | async-start | bytes 2113536
  584.7 956.4 %reduce-scatter.9.cloned.1.call-start = ((), (), s32[]{:S(2)}) async-start(), calls=%async_computation.3 | async-start | bytes 2113536
  1342.8 5.0 copy-start
Sparse Core Ops, SparseCore 0:
  584.8 193.3 reduce-scatter.6
  1348.0 193.0 reduce-scatter.8
